TPU v7x, 512 devices: a whole 4x4x16 slice. The times are simulated.
512 devices in a mesh: sa: 16 (over z_lo, core), sb: 16 (over y, x), noise: 2 (over z_hi).
Axes of the slice: x: 4, y: 4, z: 16 (z_hi: 2, z_lo: 8; z = z_hi * 8 + z_lo), core: 2. Of those that a mesh axis runs over, the one named last changes fastest.
Arguments:
- base: bfloat16 [8192, 1536], P(('sa', 'sb')), may hold values from -6 to 6
- noise: bfloat16 [4, 8192, 1536], P('noise', ('sa', 'sb')), may hold values from -3 to 3
- cot: bfloat16 [8192, 1536], P(('sa', 'sb')), may hold values from -6 to 6
- convolution_weight: bfloat16 [3, 1536, 384], P(None, 'sa'), may hold values from -0.15625 to 0.15625
- mix_w: bfloat16 [384, 1536], P('sa'), may hold values from -0.625 to 0.625
- norm_gain: float32 [1536], replicated, may hold values from 0.1 to 1.9
- qkv_w: bfloat16 [1536, 896], P('sa'), may hold values from -1 to 1
- out_w: bfloat16 [384, 1536], P('sa'), may hold values from -1.25 to 1.25
- band_width: int32 [4], replicated, may hold values from 1 to 32, as said below
- pairs: int32 [64, 2], replicated, may hold values from 0 to 63, as said below
Outputs:
- saliency: float32 [8192, 1536], P(('sa', 'sb'))
Inputs may be any that keep to these rules, and one draw needn't show every extreme that they name: `band_width`: one head has band half-width exactly 32. Tile t holds bins t * 128 to (t + 1) * 128 - 1; both tiles of a pair lie in the same stretch of 512 bins that starts at a multiple of 512; pairs may repeat.
All inputs are finite; a program needn't handle non-finite values.
Results may differ from a plain program's by a relative error of at most 0.018.
Values may be sent and summed in bfloat16 or wider, within the bound.
A program may use at most 64 MiB of HBM per device.

v0:
```python
import jax
import jax.numpy as jnp
from jax import lax
from jax.sharding import PartitionSpec as P

HID = 384
HEADS = 4
KEY = 64
VAL = 96
DILATION_BINS = 16
BAND = 32
TILE = 128


ROOT_TWO_PI = 0.7978845608
CUBIC = 0.044715


def extended(value, sides, width):
    for axis, dim in sides:
        peers, length = (lax.axis_size(axis), value.shape[dim])
        up = [(i, (i + 1) % peers) for i in range(peers - 1)]
        down = [(j, i) for i, j in up]
        last = lax.slice_in_dim(value, length - width, length, axis=dim)
        leading = lax.slice_in_dim(value, 0, width, axis=dim)
        before = lax.ppermute(last, axis, up)
        after = lax.ppermute(leading, axis, down)
        value = jnp.concatenate([before, value, after], axis=dim)
    return value


def from_behind(block, axis, distance):
    devices = range(lax.axis_size(axis))
    route = [(i - distance, i) for i in devices if i - distance in devices]
    return lax.ppermute(block, axis, route)


def gelu_tanh(values):
    inner = ROOT_TWO_PI * (values + CUBIC * values * values * values)
    return 0.5 * values * (1.0 + jnp.tanh(inner))


def gelu_slope(values):
    tangent = jnp.tanh(ROOT_TWO_PI * (values + CUBIC * values * values * values))
    return 0.5 * (1.0 + tangent) + 0.5 * values * (1.0 - tangent * tangent) * ROOT_TWO_PI * (
        1.0 + 3.0 * CUBIC * values * values
    )


def shards(base, noise, cot, convolution_weight, mix_w, norm_gain, qkv_w, out_w, band_width, pairs):
    conv_full, mix_full, qkv_full, out_full = (
        lax.all_gather(convolution_weight, "sa", axis=1, tiled=True),
        lax.all_gather(mix_w, "sa", axis=0, tiled=True),
        lax.all_gather(qkv_w, "sa", axis=0, tiled=True),
        lax.all_gather(out_w, "sa", axis=0, tiled=True),
    )
    sequence_bins = base.shape[0]
    samples_dev = noise.shape[0]
    stretch = sequence_bins * lax.axis_size("sb")
    sequence_length = stretch * lax.axis_size("sa")
    heads_key = HEADS * KEY
    heads_val = HEADS * VAL
    width = sequence_bins + 2 * BAND
    scale = KEY ** (-0.5)
    stretch_first = lax.axis_index("sa") * stretch
    first_row = stretch_first + lax.axis_index("sb") * sequence_bins
    row_pos = first_row + jnp.arange(sequence_bins, dtype=jnp.int32)
    ext_pos = first_row - BAND + jnp.arange(width, dtype=jnp.int32)
    stretch_pos = stretch_first + jnp.arange(stretch, dtype=jnp.int32)
    tiles = sequence_length // TILE
    tile_ids = jnp.arange(tiles, dtype=jnp.int32)
    pick_query = (pairs[:, 0][:, None] == tile_ids[None, :]).astype(jnp.float32)
    pick_key = (pairs[:, 1][:, None] == tile_ids[None, :]).astype(jnp.float32)
    table = jnp.dot(pick_query.T, pick_key)
    own_select = ((row_pos // TILE)[:, None] == tile_ids[None, :]).astype(jnp.float32)
    stretch_select = ((stretch_pos // TILE)[:, None] == tile_ids[None, :]).astype(jnp.float32)
    pair_own_rows = jnp.dot(jnp.dot(own_select, table), stretch_select.T) > 0.5
    pair_own_keys = jnp.dot(jnp.dot(stretch_select, table), own_select.T) > 0.5
    inside = (ext_pos >= 0) & (ext_pos < sequence_length)
    band_mask = inside[None, None, :] & (
        jnp.abs(row_pos[:, None] - ext_pos[None, :])[None] <= band_width[:, None, None]
    )
    far_rows = jnp.abs(row_pos[:, None] - stretch_pos[None, :])[None] > band_width[:, None, None]
    pair_mask = pair_own_rows[None] & far_rows
    key_mask = pair_own_keys[None] & jnp.transpose(far_rows, (0, 2, 1))
    noisy = base.astype(jnp.float32)[None] + noise.astype(jnp.float32)
    gelu_input = gelu_tanh(noisy).astype(jnp.bfloat16)
    gelu_extended = extended(gelu_input, ((("sa", "sb"), 1),), DILATION_BINS)
    hidden_state = jnp.zeros((samples_dev, sequence_bins, HID), jnp.float32)
    for tap_index in range(3):
        hidden_state = hidden_state + jnp.einsum(
            "nbd,dc->nbc",
            gelu_extended[:, tap_index * DILATION_BINS : tap_index * DILATION_BINS + sequence_bins],
            conv_full[tap_index],
            preferred_element_type=jnp.float32,
        )
    act = gelu_tanh(hidden_state).astype(jnp.bfloat16)
    resid = noisy + jnp.einsum("nbc,cd->nbd", act, mix_full, preferred_element_type=jnp.float32)
    inv_rms = lax.rsqrt(jnp.mean(resid * resid, axis=-1, keepdims=True) + 1e-06)
    normed = (resid * inv_rms * norm_gain).astype(jnp.bfloat16)
    proj = jnp.einsum("nbd,dc->nbc", normed, qkv_full, preferred_element_type=jnp.float32).astype(
        jnp.bfloat16
    )
    queries = proj[..., :heads_key].reshape(samples_dev, sequence_bins, HEADS, KEY)
    key_vals = proj[..., heads_key:]
    kv_ext = extended(key_vals, ((("sa", "sb"), 1),), BAND)
    kv_all = lax.all_gather(key_vals, "sb", axis=1, tiled=True)
    keys_ext = kv_ext[..., :heads_key].reshape(samples_dev, width, HEADS, KEY)
    vals_ext = kv_ext[..., heads_key:].reshape(samples_dev, width, HEADS, VAL)
    keys_all = kv_all[..., :heads_key].reshape(samples_dev, stretch, HEADS, KEY)
    vals_all = kv_all[..., heads_key:].reshape(samples_dev, stretch, HEADS, VAL)
    score_band = (
        jnp.einsum("nihd,njhd->nhij", queries, keys_ext, preferred_element_type=jnp.float32) * scale
    )
    score_band = jnp.where(band_mask[None], score_band, -1e30)
    raw_pair = jnp.einsum("nihd,njhd->nhij", queries, keys_all, preferred_element_type=jnp.float32)
    score_pair = jnp.where(pair_mask[None], raw_pair * scale, -1e30)
    top = jnp.maximum(jnp.max(score_band, axis=-1), jnp.max(score_pair, axis=-1))
    total = jnp.sum(jnp.where(band_mask[None], jnp.exp(score_band - top[..., None]), 0.0), axis=-1)
    total = total + jnp.sum(
        jnp.where(pair_mask[None], jnp.exp(score_pair - top[..., None]), 0.0), axis=-1
    )
    lse = top + jnp.log(total)
    prob_band = jnp.where(band_mask[None], jnp.exp(score_band - lse[..., None]), 0.0)
    prob_pair = jnp.where(pair_mask[None], jnp.exp(score_pair - lse[..., None]), 0.0)
    band_b = prob_band.astype(jnp.bfloat16)
    pair_b = prob_pair.astype(jnp.bfloat16)
    attn = jnp.einsum("nhij,njhe->nihe", band_b, vals_ext, preferred_element_type=jnp.float32)
    attn = attn + jnp.einsum(
        "nhij,njhe->nihe", pair_b, vals_all, preferred_element_type=jnp.float32
    )
    d_att = jnp.dot(cot, out_full.T, preferred_element_type=jnp.float32).astype(jnp.bfloat16)
    d_att_heads = d_att.reshape(sequence_bins, HEADS, VAL)
    delta = jnp.transpose(jnp.sum(d_att_heads.astype(jnp.float32)[None] * attn, axis=-1), (0, 2, 1))
    d_prob_band = jnp.einsum(
        "ihe,njhe->nhij", d_att_heads, vals_ext, preferred_element_type=jnp.float32
    )
    d_prob_pair = jnp.einsum(
        "ihe,njhe->nhij", d_att_heads, vals_all, preferred_element_type=jnp.float32
    )
    d_score_band = (prob_band * (d_prob_band - delta[..., None]) * scale).astype(jnp.bfloat16)
    d_score_pair = (prob_pair * (d_prob_pair - delta[..., None]) * scale).astype(jnp.bfloat16)
    d_query = jnp.einsum(
        "nhij,njhd->nihd", d_score_band, keys_ext, preferred_element_type=jnp.float32
    )
    d_query = d_query + jnp.einsum(
        "nhij,njhd->nihd", d_score_pair, keys_all, preferred_element_type=jnp.float32
    )
    d_key_ext = jnp.einsum(
        "nhij,nihd->njhd", d_score_band, queries, preferred_element_type=jnp.float32
    )
    d_val_ext = jnp.einsum(
        "nhij,ihe->njhe", band_b, d_att_heads, preferred_element_type=jnp.float32
    )
    d_kv_ext = jnp.concatenate(
        [
            d_key_ext.reshape(samples_dev, width, heads_key),
            d_val_ext.reshape(samples_dev, width, heads_val),
        ],
        axis=2,
    )
    from_right = from_behind(d_kv_ext[:, :BAND].astype(jnp.bfloat16), ("sa", "sb"), -1).astype(
        jnp.float32
    )
    from_left = from_behind(
        d_kv_ext[:, BAND + sequence_bins :].astype(jnp.bfloat16), ("sa", "sb"), 1
    ).astype(jnp.float32)
    d_key_vals = d_kv_ext[:, BAND : BAND + sequence_bins]
    d_key_vals = d_key_vals + from_left
    d_key_vals = d_key_vals + from_right
    statistics = jnp.stack([lse, delta], axis=1)
    query_rows = proj[..., :heads_key]
    queries_all, d_att_all = (
        lax.all_gather(query_rows, "sb", axis=1, tiled=True),
        lax.all_gather(d_att, "sb", axis=0, tiled=True),
    )
    stats_all = lax.all_gather(statistics, "sb", axis=3, tiled=True)
    queries_all = queries_all.reshape(samples_dev, stretch, HEADS, KEY)
    d_att_all = d_att_all.reshape(stretch, HEADS, VAL)
    keys_own = key_vals[..., :heads_key].reshape(samples_dev, sequence_bins, HEADS, KEY)
    vals_own = key_vals[..., heads_key:].reshape(samples_dev, sequence_bins, HEADS, VAL)
    score_key = (
        jnp.einsum("nihd,njhd->nhij", queries_all, keys_own, preferred_element_type=jnp.float32)
        * scale
    )
    prob_key = jnp.where(key_mask[None], jnp.exp(score_key - stats_all[:, 0][..., None]), 0.0)
    d_val_pair = jnp.einsum(
        "nhij,ihe->njhe",
        prob_key.astype(jnp.bfloat16),
        d_att_all,
        preferred_element_type=jnp.float32,
    )
    d_prob_key = jnp.einsum(
        "ihe,njhe->nhij", d_att_all, vals_own, preferred_element_type=jnp.float32
    )
    d_score_key = (prob_key * (d_prob_key - stats_all[:, 1][..., None]) * scale).astype(
        jnp.bfloat16
    )
    d_key_pair = jnp.einsum(
        "nhij,nihd->njhd", d_score_key, queries_all, preferred_element_type=jnp.float32
    )
    d_key_vals = d_key_vals + jnp.concatenate(
        [
            d_key_pair.reshape(samples_dev, sequence_bins, heads_key),
            d_val_pair.reshape(samples_dev, sequence_bins, heads_val),
        ],
        axis=2,
    )
    d_proj = jnp.concatenate(
        [d_query.reshape(samples_dev, sequence_bins, heads_key), d_key_vals], axis=2
    ).astype(jnp.bfloat16)
    d_normed = jnp.einsum("nbc,dc->nbd", d_proj, qkv_full, preferred_element_type=jnp.float32)
    gained = norm_gain * d_normed
    d_resid = (
        cot.astype(jnp.float32)[None]
        + inv_rms * gained
        - resid * inv_rms * inv_rms * inv_rms * jnp.mean(resid * gained, axis=-1, keepdims=True)
    )
    d_act = jnp.einsum(
        "nbd,cd->nbc", d_resid.astype(jnp.bfloat16), mix_full, preferred_element_type=jnp.float32
    )
    hidden_gradient = (d_act * gelu_slope(hidden_state)).astype(jnp.bfloat16)
    gradient_extended = extended(hidden_gradient, ((("sa", "sb"), 1),), DILATION_BINS)
    d_gelu_in = jnp.zeros((samples_dev, sequence_bins, base.shape[1]), jnp.float32)
    for tap_index in range(3):
        start_offset = (2 - tap_index) * DILATION_BINS
        d_gelu_in = d_gelu_in + jnp.einsum(
            "nbc,dc->nbd",
            gradient_extended[:, start_offset : start_offset + sequence_bins],
            conv_full[tap_index],
            preferred_element_type=jnp.float32,
        )
    grads = d_resid + d_gelu_in * gelu_slope(noisy)
    summed = lax.psum(jnp.sum(grads, axis=0).astype(jnp.bfloat16), "noise").astype(jnp.float32)
    return summed / (samples_dev * lax.axis_size("noise"))


def solution(mesh):
    return jax.shard_map(
        shards,
        mesh=mesh,
        in_specs=(
            P(("sa", "sb"), None),
            P("noise", ("sa", "sb"), None),
            P(("sa", "sb"), None),
            P(None, "sa", None),
            P("sa", None),
            P(),
            P("sa", None),
            P("sa", None),
            P(),
            P(),
        ),
        out_specs=P(("sa", "sb"), None),
        check_vma=False,
    )
```

profile of v0, /device:TPU:1, one launch (start us, length us, event | category | flops | bytes accessed | tf_op | source)
XLA Modules:
  0.0 632.5 jit_solution(18089078313766101049)
XLA Ops:
  8.8 0.9 convert_element_type.75
  9.7 1.2 multiply_convert_fusion.1
  10.9 8.2 %collective-permute-start.1 = (bf16[2,16,1536]{2,1,0:T(8,128)(2,1)S(1)}, bf16[2,16,1536]{2,1,0:T(8,128)(2,1)S(1)}, u32[]{:S(2)}, u32[]{:S(2)}) collective-permute-start(bf16[2,16,1536]{2,1,0:T(8,128)(2,1)S(1)} %get-tuple-element.10), channel_id=1, source_target_pairs={{2,0},{4,2},{6,4},{8,6},{10,8},{12,10},{14,12},{16,14},{18,16},{20... | collective-permute-start | bytes 294920 | tf_op jit(solution)/shard_map/ppermute | solution.py:27
  19.1 1.9 collective-permute-start
  22.6 95.0 %all-gather.6.cloned.1.call-done = bf16[3,1536,384]{2,1,0:T(8,128)(2,1)} async-done(((bf16[3,96,384]{2,1,0:T(8,128)(2,1)}), bf16[3,1536,384]{2,1,0:T(8,128)(2,1)}) %all-gather.6.cloned.1.call-update) | async-done | bytes 3538960 | tf_op jit(solution)/shard_map/all_gather | solution.py:52
  117.6 1.6 fusion.58
  119.2 1.6 fusion.60
  120.8 1.6 fusion.44
  122.4 97.1 %all-gather.8.cloned.1.call-done = bf16[384,1536]{1,0:T(8,128)(2,1)} async-done(((bf16[24,1536]{1,0:T(8,128)(2,1)}), bf16[384,1536]{1,0:T(8,128)(2,1)}) %all-gather.8.cloned.1.call-update) | async-done | bytes 1179664 | tf_op jit(solution)/shard_map/all_gather | solution.py:53
  219.5 1.7 multiply_reduce_fusion.1
  221.2 103.6 %all-gather.10.cloned.1.call-done = bf16[1536,896]{1,0:T(8,128)(2,1)} async-done(((bf16[96,896]{1,0:T(8,128)(2,1)}), bf16[1536,896]{1,0:T(8,128)(2,1)}) %all-gather.10.cloned.1.call-update) | async-done | bytes 2752528 | tf_op jit(solution)/shard_map/all_gather | solution.py:54
  324.9 2.4 fusion.28
  329.6 96.9 %all-gather.14.cloned.1.call-done = bf16[384,1536]{1,0:T(8,128)(2,1)} async-done(((bf16[24,1536]{1,0:T(8,128)(2,1)}), bf16[384,1536]{1,0:T(8,128)(2,1)}) %all-gather.14.cloned.1.call-update) | async-done | bytes 1179664 | tf_op jit(solution)/shard_map/all_gather | solution.py:55
  426.5 1.7 convolution_convert_fusion
  428.9 18.8 %all_gather.31 = bf16[512,384]{1,0:T(8,128)(2,1)S(1)} all-gather(bf16[32,384]{1,0:T(8,128)(2,1)S(1)} %convolution_convert_fusion), channel_id=1, replica_groups=mesh['sa'=16,'sb'=16,'noise'=2] {'sb'}, dimensions={0}, use_global_device_ids=true | all-gather | bytes 417792 | tf_op jit(solution)/shard_map/all_gather | solution.py:175
  447.9 2.7 collective-permute-start.2
  450.7 9.8 %collective-permute-start.3 = (bf16[2,32,640]{2,1,0:T(8,128)(2,1)S(1)}, bf16[2,32,640]{2,1,0:T(8,128)(2,1)S(1)}, u32[]{:S(2)}, u32[]{:S(2)}) collective-permute-start(bf16[2,32,640]{2,1,0:T(8,128)(2,1)S(1)} %copy-done.11), channel_id=1, source_target_pairs={{2,0},{4,2},{6,4},{8,6},{10,8},{12,10},{14,12},{16,14},{18,16},{20... | collective-permute-start | bytes 245768 | tf_op jit(solution)/shard_map/ppermute | solution.py:27
  460.6 16.1 %all_gather.29 = bf16[2,512,256]{2,1,0:T(8,128)(2,1)S(1)} all-gather(bf16[2,32,256]{2,1,0:T(8,128)(2,1)S(1)} %get-tuple-element.12), channel_id=1, replica_groups=mesh['sa'=16,'sb'=16,'noise'=2] {'sb'}, dimensions={1}, use_global_device_ids=true | all-gather | bytes 557056 | tf_op jit(solution)/shard_map/all_gather | solution.py:174
  476.9 0.8 reshape.249
  478.6 0.8 reshape.242
  479.7 9.0 %all-gather.12.cloned.1.call-done = bf16[2,512,640]{2,1,0:T(8,128)(2,1)} async-done(((bf16[2,32,640]{2,1,0:T(8,128)(2,1)}), bf16[2,512,640]{2,1,0:T(8,128)(2,1)}) %all-gather.12.cloned.1.call-update) | async-done | bytes 1310736 | tf_op jit(solution)/shard_map/all_gather | solution.py:107
  488.7 1.0 slice-done
  490.3 0.8 select_reduce_fusion
  491.1 0.8 select_reduce_fusion.1
  493.0 1.3 fusion.70
  494.3 0.9 fusion.50
  495.3 1.9 fusion.26
  497.2 1.0 fusion.45
  499.1 19.1 %all_gather.30 = f32[2,2,4,512]{2,1,0,3:T(2,128)S(1)} all-gather(f32[2,2,4,32]{2,1,0,3:T(2,128)S(1)} %copy.131), channel_id=1, replica_groups=mesh['sa'=16,'sb'=16,'noise'=2] {'sb'}, dimensions={3}, use_global_device_ids=true | all-gather | bytes 34816 | tf_op jit(solution)/shard_map/all_gather | solution.py:177
  518.1 0.8 fusion.150
  519.2 0.8 copy.135
  521.9 2.0 collective-permute-start.4
  523.9 10.6 %collective-permute-start.5 = (bf16[2,32,640]{2,1,0:T(8,128)(2,1)}, bf16[2,32,640]{2,1,0:T(8,128)(2,1)}, u32[]{:S(2)}, u32[]{:S(2)}) collective-permute-start(bf16[2,32,640]{2,1,0:T(8,128)(2,1)} %get-tuple-element.8), channel_id=1, source_target_pairs={{2,0},{4,2},{6,4},{8,6},{10,8},{12,10},{14,12},{16,14},{18,16},{20... | collective-permute-start | bytes 245768 | tf_op jit(solution)/shard_map/ppermute | solution.py:35
  534.6 1.1 fusion.157
  535.6 0.9 convolution_bitcast_fusion.3
  536.5 2.5 fusion.31
  539.0 1.2 fusion.51
  541.0 1.6 copy.136
  542.6 1.7 reshape.252
  544.3 1.6 copy.138
  545.9 1.0 reshape.253
  547.0 1.1 fusion.94
  548.2 2.0 multiply_reduce_fusion
  550.7 1.9 collective-permute-start.7
  552.6 7.0 %collective-permute-start.6 = (bf16[2,16,384]{2,1,0:T(8,128)(2,1)S(1)}, bf16[2,16,384]{2,1,0:T(8,128)(2,1)S(1)}, u32[]{:S(2)}, u32[]{:S(2)}) collective-permute-start(bf16[2,16,384]{2,1,0:T(8,128)(2,1)S(1)} %get-tuple-element.13), channel_id=1, source_target_pairs={{2,0},{4,2},{6,4},{8,6},{10,8},{12,10},{14,12},{16,14},{18,16},{20... | collective-permute-start | bytes 73736 | tf_op jit(solution)/shard_map/ppermute | solution.py:27
  561.1 1.3 fusion.25
  562.4 61.6 %all-reduce.2.cloned.1.call-done = bf16[32,1536]{1,0:T(8,128)(2,1)} async-done(((bf16[32,1536]{1,0:T(8,128)(2,1)}), bf16[32,1536]{1,0:T(8,128)(2,1)}) %all-reduce.2.cloned.1.call-update) | async-done | bytes 98320 | tf_op jit(solution)/shard_map/psum | solution.py:234
  624.0 1.6 convert_multiply_fusion
  (158 shorter events, 15.6 us)
Async XLA Ops:
  6.5 14.7 %copy-start.40 = (s32[64,2]{0,1:T(2,128)S(1)}, s32[64,2]{0,1:T(2,128)}, u32[]{:S(2)}) copy-start(s32[64,2]{0,1:T(2,128)} %param.19) | copy-start | bytes 1540
  6.5 14.7 %copy-start.24 = (bf16[32,1536]{1,0:T(8,128)(2,1)S(1)}, bf16[32,1536]{1,0:T(8,128)(2,1)}, u32[]{:S(2)}) copy-start(bf16[32,1536]{1,0:T(8,128)(2,1)} %param.12) | copy-start | bytes 294916
  6.5 111.0 %all-gather.6.cloned.1.call-start = ((), (), s32[]{:S(2)}) async-start(), calls=%async_computation | async-start | bytes 3760128 | tf_op jit(solution)/shard_map/all_gather | solution.py:52
  7.3 212.3 %all-gather.8.cloned.1.call-start = ((), (), s32[]{:S(2)}) async-start(), calls=%async_computation.1 | async-start | bytes 1253376 | tf_op jit(solution)/shard_map/all_gather | solution.py:53
  8.0 316.8 %all-gather.10.cloned.1.call-start = ((), (), s32[]{:S(2)}) async-start(), calls=%async_computation.2 | async-start | bytes 2924544 | tf_op jit(solution)/shard_map/all_gather | solution.py:54
  8.7 417.7 %all-gather.14.cloned.1.call-start = ((), (), s32[]{:S(2)}) async-start(), calls=%async_computation.4 | async-start | bytes 1253376 | tf_op jit(solution)/shard_map/all_gather | solution.py:55
  9.7 209.8 %copy-start.8 = (f32[32,1536]{1,0:T(8,128)}, f32[32,1536]{1,0:T(8,128)S(1)}, u32[]{:S(2)}) copy-start(f32[32,1536]{1,0:T(8,128)S(1)} %convert_element_type.75) | copy-start | bytes 589828
  10.9 108.3 %collective-permute-start.1 = (bf16[2,16,1536]{2,1,0:T(8,128)(2,1)S(1)}, bf16[2,16,1536]{2,1,0:T(8,128)(2,1)S(1)}, u32[]{:S(2)}, u32[]{:S(2)}) collective-permute-start(bf16[2,16,1536]{2,1,0:T(8,128)(2,1)S(1)} %get-tuple-element.10), channel_id=1, source_target_pairs={{2,0},{4,2},{6,4},{8,6},{10,8},{12,10},{14,12},{16,14},{18,16},{20... | collective-permute-start | bytes 294920 | tf_op jit(solution)/shard_map/ppermute | solution.py:27
  19.1 101.7 %collective-permute-start = (bf16[2,16,1536]{2,1,0:T(8,128)(2,1)S(1)}, bf16[2,16,1536]{2,1,0:T(8,128)(2,1)S(1)}, u32[]{:S(2)}, u32[]{:S(2)}) collective-permute-start(bf16[2,16,1536]{2,1,0:T(8,128)(2,1)S(1)} %get-tuple-element.9), channel_id=1, source_target_pairs={{0,2},{2,4},{4,6},{6,8},{8,10},{10,12},{12,14},{14,16},{16,18},{18... | collective-permute-start | bytes 294920 | tf_op jit(solution)/shard_map/ppermute | solution.py:26
  21.1 467.6 %all-gather.12.cloned.1.call-start = ((), (), s32[]{:S(2)}) async-start(), calls=%async_computation.3 | async-start | bytes 1392640 | tf_op jit(solution)/shard_map/all_gather | solution.py:107
  120.8 98.8 %copy-start.20 = (bf16[2,32,1536]{2,1,0:T(8,128)(2,1)S(1)}, bf16[2,32,1536]{2,1,0:T(8,128)(2,1)}, u32[]{:S(2)}) copy-start(bf16[2,32,1536]{2,1,0:T(8,128)(2,1)} %param.11) | copy-start | bytes 589828
  122.4 204.9 %copy-start.17 = (f32[2,32,384]{2,1,0:T(8,128)}, f32[2,32,384]{2,1,0:T(8,128)S(1)}, u32[]{:S(2)}) copy-start(f32[2,32,384]{2,1,0:T(8,128)S(1)} %fusion.44) | copy-start | bytes 294916
  122.4 202.4 %copy-start.31 = (f32[1536]{0:T(1024)S(1)}, f32[1536]{0:T(1024)}, u32[]{:S(2)}) copy-start(f32[1536]{0:T(1024)} %param.15) | copy-start | bytes 18436
  221.2 106.1 %copy-start.37 = (f32[2,32]{1,0:T(2,128)}, f32[2,32]{1,0:T(2,128)S(1)}, u32[]{:S(2)}) copy-start(f32[2,32]{1,0:T(2,128)S(1)} %add_rsqrt_fusion) | copy-start | bytes 772
  324.9 3.2 copy-start.39
  327.3 133.1 %copy-start.19 = (bf16[2,32,896]{2,1,0:T(8,128)(2,1)}, bf16[2,32,896]{2,1,0:T(8,128)(2,1)S(1)}, u32[]{:S(2)}) copy-start(bf16[2,32,896]{2,1,0:T(8,128)(2,1)S(1)} %fusion.28) | copy-start | bytes 344068
  328.0 296.1 %all-reduce.2.cloned.1.call-start = ((), (), s32[]{:S(2)}) async-start(), calls=%async_computation.5 | async-start | bytes 196608 | tf_op jit(solution)/shard_map/psum | solution.py:234
  328.9 161.4 %copy-start.13 = (pred[4,32,512]{2,1,0:T(8,128)(4,1)}, pred[4,32,512]{2,1,0:T(8,128)(4,1)S(1)}, u32[]{:S(2)}) copy-start(pred[4,32,512]{2,1,0:T(8,128)(4,1)S(1)} %compare_and_fusion.1) | copy-start | bytes 196612
  329.6 118.3 %copy-start.11 = (bf16[2,32,640]{2,1,0:T(8,128)(2,1)S(1)}, bf16[2,32,640]{2,1,0:T(8,128)(2,1)}, u32[]{:S(2)}) copy-start(bf16[2,32,640]{2,1,0:T(8,128)(2,1)} %slice.121) | copy-start | bytes 245764
  428.3 19.4 %copy-start.25 = (bf16[32,4,96]{2,1,0:T(4,128)(2,1)}, bf16[32,4,96]{2,1,0:T(4,128)(2,1)S(1)}, u32[]{:S(2)}) copy-start(bf16[32,4,96]{2,1,0:T(4,128)(2,1)S(1)} %reshape.243) | copy-start | bytes 73732
  447.9 30.5 %collective-permute-start.2 = (bf16[2,32,640]{2,1,0:T(8,128)(2,1)S(1)}, bf16[2,32,640]{2,1,0:T(8,128)(2,1)S(1)}, u32[]{:S(2)}, u32[]{:S(2)}) collective-permute-start(bf16[2,32,640]{2,1,0:T(8,128)(2,1)S(1)} %copy-done.11), channel_id=1, source_target_pairs={{0,2},{2,4},{4,6},{6,8},{8,10},{10,12},{12,14},{14,16},{16,18},{18... | collective-permute-start | bytes 245768 | tf_op jit(solution)/shard_map/ppermute | solution.py:26
  450.7 27.8 %collective-permute-start.3 = (bf16[2,32,640]{2,1,0:T(8,128)(2,1)S(1)}, bf16[2,32,640]{2,1,0:T(8,128)(2,1)S(1)}, u32[]{:S(2)}, u32[]{:S(2)}) collective-permute-start(bf16[2,32,640]{2,1,0:T(8,128)(2,1)S(1)} %copy-done.11), channel_id=1, source_target_pairs={{2,0},{4,2},{6,4},{8,6},{10,8},{12,10},{14,12},{16,14},{18,16},{20... | collective-permute-start | bytes 245768 | tf_op jit(solution)/shard_map/ppermute | solution.py:27
  460.5 17.2 %slice-start.2 = ((bf16[2,32,896]{2,1,0:T(8,128)(2,1)}), bf16[2,32,384]{2,1,0:T(8,128)(2,1)S(1)}, s32[]{:S(2)}) async-start(bf16[2,32,896]{2,1,0:T(8,128)(2,1)} %copy-done.19), calls=%async_computation.8 | async-start | bytes 98304 | tf_op jit(solution)/shard_map/slice | solution.py:181
  460.6 29.4 %copy-start.15 = (bf16[2,32,4,64]{3,2,1,0:T(4,128)(2,1)}, bf16[2,32,4,64]{3,2,1,0:T(4,128)(2,1)S(1)}, u32[]{:S(2)}) copy-start(bf16[2,32,4,64]{3,2,1,0:T(4,128)(2,1)S(1)} %reshape.240) | copy-start | bytes 98308
  476.9 57.6 %copy-start.2 = (bf16[2,512,256]{1,2,0:T(8,128)(2,1)}, bf16[2,512,256]{1,2,0:T(8,128)(2,1)S(1)}, u32[]{:S(2)}) copy-start(bf16[2,512,256]{1,2,0:T(8,128)(2,1)S(1)} %copy.129) | copy-start | bytes 1572868
  478.6 11.4 %copy-start.12 = (bf16[2,96,256]{1,2,0:T(8,128)(2,1)}, bf16[2,96,256]{1,2,0:T(8,128)(2,1)S(1)}, u32[]{:S(2)}) copy-start(bf16[2,96,256]{1,2,0:T(8,128)(2,1)S(1)} %copy.113) | copy-start | bytes 294916
  492.2 2.1 copy-start.22
  492.2 2.1 copy-start.29
  492.2 3.0 copy-start.7
  492.3 3.0 copy-start.14
  493.0 2.2 copy-start.33
  498.2 21.8 %copy-start.30 = (bf16[2,4,32,96]{3,2,1,0:T(8,128)(2,1)}, bf16[2,4,32,96]{3,2,1,0:T(8,128)(2,1)S(1)}, u32[]{:S(2)}) copy-start(bf16[2,4,32,96]{3,2,1,0:T(8,128)(2,1)S(1)} %fusion.45) | copy-start | bytes 147460
  520.7 13.9 %copy-start.27 = (pred[4,512,32]{1,2,0:T(8,128)(4,1)S(1)}, pred[4,512,32]{1,2,0:T(8,128)(4,1)}, u32[]{:S(2)}) copy-start(pred[4,512,32]{1,2,0:T(8,128)(4,1)} %compare_and_fusion) | copy-start | bytes 196612
  520.7 13.9 %copy-start.28 = (bf16[2,32,4,64]{3,2,1,0:T(4,128)(2,1)S(1)}, bf16[2,32,4,64]{3,2,1,0:T(4,128)(2,1)}, u32[]{:S(2)}) copy-start(bf16[2,32,4,64]{3,2,1,0:T(4,128)(2,1)} %reshape.249) | copy-start | bytes 98308
  521.1 14.5 %copy-start.4 = (f32[2,96,384]{2,1,0:T(8,128)}, f32[2,96,384]{2,1,0:T(8,128)S(1)}, u32[]{:S(2)}) copy-start(f32[2,96,384]{2,1,0:T(8,128)S(1)} %reshape.247) | copy-start | bytes 884740
  521.9 14.7 %copy-start.35 = (f32[2,4,512]{2,1,0:T(4,128)S(1)}, f32[2,4,512]{2,1,0:T(4,128)}, u32[]{:S(2)}) copy-start(f32[2,4,512]{2,1,0:T(4,128)} %copy.135) | copy-start | bytes 49156
  521.9 25.1 %collective-permute-start.4 = (bf16[2,32,640]{2,1,0:T(8,128)(2,1)}, bf16[2,32,640]{2,1,0:T(8,128)(2,1)}, u32[]{:S(2)}, u32[]{:S(2)}) collective-permute-start(bf16[2,32,640]{2,1,0:T(8,128)(2,1)} %get-tuple-element.7), channel_id=1, source_target_pairs={{0,2},{2,4},{4,6},{6,8},{8,10},{10,12},{12,14},{14,16},{16,18},{18... | collective-permute-start | bytes 245768 | tf_op jit(solution)/shard_map/ppermute | solution.py:35
  523.9 23.1 %collective-permute-start.5 = (bf16[2,32,640]{2,1,0:T(8,128)(2,1)}, bf16[2,32,640]{2,1,0:T(8,128)(2,1)}, u32[]{:S(2)}, u32[]{:S(2)}) collective-permute-start(bf16[2,32,640]{2,1,0:T(8,128)(2,1)} %get-tuple-element.8), channel_id=1, source_target_pairs={{2,0},{4,2},{6,4},{8,6},{10,8},{12,10},{14,12},{16,14},{18,16},{20... | collective-permute-start | bytes 245768 | tf_op jit(solution)/shard_map/ppermute | solution.py:35
  536.5 11.6 %copy-start = (bf16[1536,896]{1,0:T(8,128)(2,1)S(1)}, bf16[1536,896]{1,0:T(8,128)(2,1)}, u32[]{:S(2)}) copy-start(bf16[1536,896]{1,0:T(8,128)(2,1)} %all-gather.10.cloned.1.call-done) | copy-start | bytes 8257540
  539.0 8.0 %copy-start.5 = (f32[2,96,384]{2,1,0:T(8,128)S(1)}, f32[2,96,384]{2,1,0:T(8,128)}, u32[]{:S(2)}) copy-start(f32[2,96,384]{2,1,0:T(8,128)} %copy-done.4) | copy-start | bytes 884740
  539.0 9.1 %copy-start.32 = (f32[1536]{0:T(1024)S(1)}, f32[1536]{0:T(1024)}, u32[]{:S(2)}) copy-start(f32[1536]{0:T(1024)} %param.15) | copy-start | bytes 18436
  547.0 3.1 copy-start.18
  547.0 3.1 copy-start.23
  547.0 3.1 copy-start.38
  548.1 2.0 copy-start.1
  548.1 11.5 %copy-start.3 = (bf16[3,1536,384]{2,1,0:T(8,128)(2,1)S(1)}, bf16[3,1536,384]{2,1,0:T(8,128)(2,1)}, u32[]{:S(2)}) copy-start(bf16[3,1536,384]{2,1,0:T(8,128)(2,1)} %all-gather.6.cloned.1.call-done) | copy-start | bytes 10616836
  550.7 9.4 %collective-permute-start.7 = (bf16[2,16,384]{2,1,0:T(8,128)(2,1)S(1)}, bf16[2,16,384]{2,1,0:T(8,128)(2,1)S(1)}, u32[]{:S(2)}, u32[]{:S(2)}) collective-permute-start(bf16[2,16,384]{2,1,0:T(8,128)(2,1)S(1)} %get-tuple-element.14), channel_id=1, source_target_pairs={{0,2},{2,4},{4,6},{6,8},{8,10},{10,12},{12,14},{14,16},{16,18},{18... | collective-permute-start | bytes 73736 | tf_op jit(solution)/shard_map/ppermute | solution.py:26
  552.6 8.0 %collective-permute-start.6 = (bf16[2,16,384]{2,1,0:T(8,128)(2,1)S(1)}, bf16[2,16,384]{2,1,0:T(8,128)(2,1)S(1)}, u32[]{:S(2)}, u32[]{:S(2)}) collective-permute-start(bf16[2,16,384]{2,1,0:T(8,128)(2,1)S(1)} %get-tuple-element.13), channel_id=1, source_target_pairs={{2,0},{4,2},{6,4},{8,6},{10,8},{12,10},{14,12},{16,14},{18,16},{20... | collective-permute-start | bytes 73736 | tf_op jit(solution)/shard_map/ppermute | solution.py:27
  (10 other events, 13.8 us)
Sparse Core Ops, SparseCore 0:
  9.4 108.0 all-gather.5
  119.6 99.8 all-gather.7
  221.6 103.1 all-gather.9
  326.8 99.6 all-gather.13
  429.3 59.3 all-gather.11
  562.6 61.4 all-reduce.1
where the time goes:
time: 634 us; the launch traced here: 632 us
  waiting for transfers between devices  465 us (73%)
  blocking collectives  53.9 us (9%)
  starting transfers between devices  44.4 us (7%)
  matrix products  28.2 us (4%)
  local copies, waits for them, and re-layouts  16.6 us (3%)
  between operations  14.4 us (2%)
  other arithmetic  9.81 us (2%)
    all_gather x1, waiting for transfers between devices, shards(): lax.all_gather(qkv_w, 'sa', axis=0, tiled=True)  104 us
    all_gather x1, waiting for transfers between devices, shards(): lax.all_gather(mix_w, 'sa', axis=0, tiled=True)  97.1 us
    all_gather x1, waiting for transfers between devices, shards(): lax.all_gather(out_w, 'sa', axis=0, tiled=True)  96.9 us
    all_gather x1, waiting for transfers between devices, shards(): lax.all_gather(convolution_weight, 'sa', axis=1, tiled=True)  95 us
    psum x1, waiting for transfers between devices, shards(): lax.psum(jnp.sum(grads, axis=0).astype(jnp.bfloat16), 'noise')  61.6 us
    ppermute x3, starting transfers between devices, extended(): after = lax.ppermute(leading, axis, down)  25 us
    all_gather x1, blocking collectives, shards(): stats_all = lax.all_gather(statistics, 'sb', axis=3, tiled=True)  19.1 us
    all_gather x1, blocking collectives, shards(): lax.all_gather(d_att, 'sb', axis=0, tiled=True)  18.8 us
  transfers between devices with their start and end apart: 14, of which 6 were waited for; matrix products, arithmetic and copies ran while one was open for 5% of the time, Pallas kernels for 0%

commit v1 on v0

v1 whole, which is shorter than its diff:
```python
import functools

import jax
import jax.numpy as jnp
from jax import lax
from jax.experimental import pallas as pl
from jax.experimental.pallas import tpu as pltpu
from jax.sharding import PartitionSpec as P

MESH = pl.DeviceIdType.MESH
D = 1536
HID = 384
HEADS = 4
KEY = 64
VAL = 96
HK = HEADS * KEY
HV = HEADS * VAL
QKV = 2 * HK + HV
DIL = 16
BAND = 32
TILE = 128
BINS = 32
NS = 2
ROWS = NS * BINS
STRETCH = 512
LENGTH = 8192
CELLS = 640
SA = 16
LAST = 15
ROOT_TWO_PI = 0.7978845608
CUBIC = 0.044715
F32 = jnp.float32
BF16 = jnp.bfloat16
Z_STEPS = (1, -1, 2, -2, 3, -3, 4)
NSEM = 200


def gelu_and_slope(v):
    tangent = jnp.tanh(ROOT_TWO_PI * (v + CUBIC * v * v * v))
    half = 0.5 * (1.0 + tangent)
    slope = half + 0.5 * v * (1.0 - tangent * tangent) * ROOT_TWO_PI * (1.0 + 3.0 * CUBIC * v * v)
    return v * half, slope


def dot(a, b):
    return lax.dot_general(a, b, (((1,), (0,)), ((), ())), preferred_element_type=F32)


def dot_t(a, b):
    return lax.dot_general(a, b, (((1,), (1,)), ((), ())), preferred_element_type=F32)


def dot_l(a, b):
    return lax.dot_general(a, b, (((0,), (0,)), ((), ())), preferred_element_type=F32)


def lane_heads(value, width):
    lanes = lax.broadcasted_iota(jnp.int32, value.shape, 1)
    return [jnp.where((lanes >= h * width) & (lanes < (h + 1) * width), value, jnp.zeros_like(value)) for h in range(HEADS)]


def stack_heads(value, width):
    return jnp.concatenate(lane_heads(value, width), axis=0)


def unstack_heads(value, width):
    rows = value.shape[0] // HEADS
    lanes = lax.broadcasted_iota(jnp.int32, (rows, value.shape[1]), 1)
    total = jnp.zeros((rows, value.shape[1]), F32)
    for h in range(HEADS):
        part = value[h * rows : (h + 1) * rows]
        total = total + jnp.where((lanes >= h * width) & (lanes < (h + 1) * width), part, 0.0)
    return total


def kernel(
    base_ref, noise_ref, cot_ref, conv_ref, mix_ref, gain_ref, qkv_ref, outw_ref, bw_ref, pairs_ref,
    out_ref,
    base_v, noise_v, cot_v, noisy_v, slope_v, gext, conv_v, mix_v, qkv_v, outw_v,
    resid_v, proj_v, datt_v, stat_v, mask_q, mask_k, hgext, sum_v, far_v,
    ssem, rsem, lsem,
):
    sa, sb, hi = lax.axis_index("sa"), lax.axis_index("sb"), lax.axis_index("noise")
    zl, core = sa // 2, sa % 2
    y, x = sb // 4, sb % 4
    zf = hi * 8 + zl
    me = (sa, sb, hi)

    def at_z(d):
        z = (zf + d + 16) % 16
        return ((z % 8) * 2 + core, sb, z // 8)

    sibling = (zl * 2 + 1 - core, sb, hi)
    partner = (sa, sb, 1 - hi)

    def at_x(d):
        return (sa, y * 4 + (x + d + 4) % 4, hi)

    def at_y(d):
        return (sa, ((y + d + 4) % 4) * 4 + x, hi)

    cell = sa * 16 + sb
    left_cell, right_cell = cell - 1, cell + 1
    has_left, has_right = cell > 0, cell < 255
    left = ((left_cell + 256) % 256 // 16, (left_cell + 256) % 16, hi)
    right = (right_cell % 256 // 16, right_cell % 16, hi)
    edge_left = (sb == 0) & (sa > 0)
    edge_right = (sb == LAST) & (sa < SA - 1)

    count = [0]
    pending = []

    def remote(src, dst, device):
        n = count[0]
        count[0] += 1
        return pltpu.make_async_remote_copy(
            src_ref=src, dst_ref=dst, send_sem=ssem.at[n], recv_sem=rsem.at[n], device_id=device, device_id_type=MESH
        )

    def send(src, dst, device):
        copy = remote(src, dst, device)
        copy.start()
        pending.append(copy)
        return copy

    local = []

    def fetch(src, dst):
        copy = pltpu.make_async_copy(src, dst, lsem.at[len(local)])
        copy.start()
        local.append(copy)
        return copy

    got_base = fetch(base_ref, base_v)
    got_noise = fetch(noise_ref, noise_v)
    got_cot = fetch(cot_ref, cot_v)

    def cols(p):
        return pl.ds(pl.multiple_of(p * 384, 128), 384)

    def rows(p):
        return pl.ds(pl.multiple_of(p * 24, 8), 24)

    def conv_item(tap, first, width):
        c = pl.ds(first, width)
        return (
            lambda p: conv_ref.at[tap, rows(p), c],
            lambda z, k, p: conv_v.at[tap, z, k, p, :, c],
        )

    def qkv_item(first, width):
        c = pl.ds(first, width)
        return (lambda p: qkv_ref.at[rows(p), c], lambda z, k, p: qkv_v.at[z, k, p, :, c])

    def col_item(source, gathered):
        return (lambda p: source.at[:, cols(p)], lambda z, k, p: gathered.at[z, k, :, cols(p)])

    def col_all(gathered):
        return lambda k: gathered.at[:, k]

    every = pl.ds(0, 8)
    low, high = pl.ds(0, 4), pl.ds(4, 4)
    items = [
        (conv_item(0, 0, 384), "x", lambda k: conv_v.at[0, :, k]),
        (conv_item(2, 0, 384), "y", lambda k: conv_v.at[2, :, k]),
        (conv_item(1, 0, 256), "x", lambda k: conv_v.at[1, :, k, :, :, pl.ds(0, 256)]),
        (conv_item(1, 256, 128), "y", lambda k: conv_v.at[1, :, k, :, :, pl.ds(256, 128)]),
        (col_item(mix_ref, mix_v), "y", col_all(mix_v)),
        (qkv_item(512, 384), "x", lambda k: qkv_v.at[:, k, :, :, pl.ds(512, 384)]),
        (qkv_item(0, 512), "y", lambda k: qkv_v.at[:, k, :, :, pl.ds(0, 512)]),
        (col_item(outw_ref, outw_v), "x", col_all(outw_v)),
    ]
    own_piece = []
    for (source, slot), route, _ in items:
        p = x if route == "x" else y
        own_piece.append(fetch(source(p), slot(zl, core, p)))

    barrier = pltpu.get_barrier_semaphore()
    peers = [at_z(d) for d in (1, -1, 2, -2, 3, -3, 4, -4)] + [sibling, partner]
    for dy in range(4):
        for dx in range(4):
            if dy or dx:
                peers.append((sa, ((y + dy) % 4) * 4 + (x + dx) % 4, hi))
    for device in peers:
        pl.semaphore_signal(barrier, inc=1, device_id=device, device_id_type=MESH)

    @pl.when(edge_left)
    def _():
        pl.semaphore_signal(barrier, inc=1, device_id=left, device_id_type=MESH)

    @pl.when(edge_right)
    def _():
        pl.semaphore_signal(barrier, inc=1, device_id=right, device_id_type=MESH)

    pl.semaphore_wait(barrier, len(peers) + jnp.where(edge_left | edge_right, 1, 0).astype(jnp.int32))

    z_copies = []
    for (source, slot), route, _ in items:
        p = x if route == "x" else y
        z_copies.append([send(source(p), slot(zl, core, p), at_z(d)) for d in Z_STEPS])

    got_base.wait()
    got_noise.wait()
    for n in range(NS):
        noisy = base_v[...].astype(F32) + noise_v[n].astype(F32)
        noisy_v[pl.ds(n * BINS, BINS), :] = noisy
        gelu, slope = gelu_and_slope(noisy)
        gext[n, pl.ds(DIL, BINS), :] = gelu.astype(BF16)
        slope_v[pl.ds(n * BINS, BINS), :] = slope

    def edge_copy(src, dst, device, condition):
        copy = remote(src, dst, device)

        @pl.when(condition)
        def _():
            copy.start()

        return copy

    def edge_wait(copy, sent, received):
        @pl.when(received)
        def _():
            copy.wait_recv()

        @pl.when(sent)
        def _():
            copy.wait_send()

    halo_l = edge_copy(gext.at[:, pl.ds(DIL, DIL), :], gext.at[:, pl.ds(DIL + BINS, DIL), :], left, has_left)
    halo_r = edge_copy(gext.at[:, pl.ds(BINS, DIL), :], gext.at[:, pl.ds(0, DIL), :], right, has_right)

    @pl.when(jnp.logical_not(has_left))
    def _():
        gext[:, pl.ds(0, DIL), :] = jnp.zeros((NS, DIL, D), BF16)
        hgext[:, pl.ds(0, DIL), :] = jnp.zeros((NS, DIL, HID), BF16)

    @pl.when(jnp.logical_not(has_right))
    def _():
        gext[:, pl.ds(DIL + BINS, DIL), :] = jnp.zeros((NS, DIL, D), BF16)
        hgext[:, pl.ds(DIL + BINS, DIL), :] = jnp.zeros((NS, DIL, HID), BF16)

    def clear(slot):
        proj_v[:, 4, slot] = jnp.zeros((NS, BINS, QKV), BF16)
        datt_v[4, slot] = jnp.zeros((BINS, HV), BF16)
        stat_v[4, slot] = jnp.zeros((8, 128), F32)

    clear(2)
    clear(3)

    @pl.when(jnp.logical_not(edge_left))
    def _():
        clear(0)

    @pl.when(jnp.logical_not(edge_right))
    def _():
        clear(1)

    first_row = cell * BINS
    first_col = sa * STRETCH
    tile_own = sa * 4 + sb // 4
    p0, p1 = pairs_ref[:, 0:1], pairs_ref[:, 1:2]

    def flag(a, b):
        return jnp.max(jnp.where((p0 == a) & (p1 == b), 1.0, 0.0), axis=0, keepdims=True)

    def band_of(index):
        wide = jnp.full(index.shape, bw_ref[0], jnp.int32)
        for h in range(1, HEADS):
            wide = jnp.where(index // BINS == h, bw_ref[h], wide)
        return wide

    def mask_of(shape, cells_dim, flags):
        r = lax.broadcasted_iota(jnp.int32, shape, cells_dim)
        hi_ = lax.broadcasted_iota(jnp.int32, shape, 1 - cells_dim)
        away = jnp.where(r < 512, r, jnp.where(r < 544, r - 544, r - 32))
        pos = first_col + away
        valid = (r < 576) & (pos >= 0) & (pos < LENGTH)
        own = first_row + hi_ % BINS
        in_band = jnp.abs(pos - own) <= band_of(hi_)
        paired = jnp.zeros(shape, F32)
        for t in range(4):
            paired = jnp.where((r >= t * TILE) & (r < (t + 1) * TILE), jnp.broadcast_to(flags[t], shape), paired)
        return jnp.where(valid & (in_band | (paired > 0.5)), 1.0, 0.0)

    mask_q[...] = mask_of((CELLS, 128), 0, [flag(tile_own, sa * 4 + t) for t in range(4)])
    mask_k[...] = mask_of((128, CELLS), 1, [flag(sa * 4 + t, tile_own) for t in range(4)])

    def ring(view, halves, index, device):
        right_copy = send(view(index), view(index), device(1))
        left_copy = send(view(index), view(index), device(-1))

        def forward():
            right_copy.wait_recv()
            a = send(halves((index + 3) % 4, 0), halves((index + 3) % 4, 0), device(1))
            left_copy.wait_recv()
            b = send(halves((index + 1) % 4, 1), halves((index + 1) % 4, 1), device(-1))

            def finish():
                a.wait_recv()
                b.wait_recv()

            return finish

        return forward

    swaps = [None] * len(items)
    forwards = [None] * len(items)
    finishes = [None] * len(items)

    def stage_a(i):
        (source, slot), route, _ = items[i]
        own_piece[i].wait()
        for copy in z_copies[i]:
            copy.wait_recv()
        forwards[i] = ring(
            lambda p: slot(every, core, p),
            lambda p, half: slot(low if half == 0 else high, core, p),
            x if route == "x" else y,
            at_x if route == "x" else at_y,
        )

    def stage_b(i):
        finishes[i] = forwards[i]()

    def stage_c(i):
        finishes[i]()
        whole = items[i][2]
        swaps[i] = send(whole(core), whole(core), sibling)

    stage_a(0)
    stage_a(1)
    stage_a(2)
    stage_a(3)
    stage_b(0)
    stage_b(1)
    stage_a(4)
    stage_b(2)
    stage_b(3)
    stage_c(0)
    stage_c(1)
    stage_a(5)
    stage_a(6)
    stage_b(4)
    stage_c(2)
    stage_c(3)
    stage_a(7)
    stage_b(5)
    stage_b(6)
    stage_c(4)

    edge_wait(halo_r, has_right, has_left)
    edge_wait(halo_l, has_left, has_right)

    def tap_of(ref, t):
        return ref[:, pl.ds(t * DIL, BINS), :].reshape(ROWS, ref.shape[2])

    swaps[0].wait_recv()
    hidden = dot(tap_of(gext, 0), conv_v[0].reshape(D, HID))
    stage_b(7)
    swaps[1].wait_recv()
    hidden = hidden + dot(tap_of(gext, 2), conv_v[2].reshape(D, HID))
    stage_c(5)
    stage_c(6)
    swaps[2].wait_recv()
    swaps[3].wait_recv()
    hidden = hidden + dot(tap_of(gext, 1), conv_v[1].reshape(D, HID))
    act, hidden_slope = gelu_and_slope(hidden)
    stage_c(7)
    swaps[4].wait_recv()
    resid = noisy_v[...] + dot(act.astype(BF16), mix_v[...].reshape(HID, D))
    resid_v[...] = resid
    inv_rms = lax.rsqrt(jnp.mean(resid * resid, axis=1, keepdims=True) + 1e-06)
    gain = gain_ref[...]
    normed = (resid * inv_rms * gain).astype(BF16)
    swaps[5].wait_recv()
    swaps[6].wait_recv()
    proj = dot(normed, qkv_v[...].reshape(D, QKV)).astype(BF16)
    for n in range(NS):
        proj_v[n, y, x] = proj[n * BINS : (n + 1) * BINS]

    def gather(ref_of, split):
        def first(n):
            def view(i):
                return ref_of(n, y, i, None) if n == 0 else ref_of(n, i, x, None)

            def halves(i, half):
                return ref_of(n, y, i, half) if n == 0 else ref_of(n, i, x, half)

            return ring(view, halves, x if n == 0 else y, at_x if n == 0 else at_y)

        def second(n):
            def view(i):
                return ref_of(n, i, pl.ds(0, 4), None) if n == 0 else ref_of(n, pl.ds(0, 4), i, None)

            def halves(i, half):
                part = pl.ds(2 * half, 2)
                return ref_of(n, i, part, None) if n == 0 else ref_of(n, part, i, None)

            return ring(view, halves, y if n == 0 else x, at_y if n == 0 else at_x)

        return first, second

    def span(rows_, half):
        return pl.ds(0, rows_) if half is None else pl.ds(half * (rows_ // 2), rows_ // 2)

    def kv_ref(n, i, j, half):
        return proj_v.at[n, i, j, span(BINS, half), pl.ds(HK, HK + HV)]

    def q_ref(n, i, j, half):
        return proj_v.at[n, i, j, span(BINS, half), pl.ds(0, HK)]

    def d_ref(n, i, j, half):
        quarter = pl.ds(n * 16, 16) if half is None else pl.ds(n * 16 + half * 8, 8)
        return datt_v.at[i, j, quarter, :]

    kv_first, kv_second = gather(kv_ref, None)
    q_first, q_second = gather(q_ref, None)
    d_first, d_second = gather(d_ref, None)

    kv_f = [kv_first(0), kv_first(1)]
    ext_l = edge_copy(proj_v.at[:, y, x], proj_v.at[:, 4, 1], left, edge_left)
    ext_r = edge_copy(proj_v.at[:, y, x], proj_v.at[:, 4, 0], right, edge_right)
    kv_g = [f() for f in kv_f]

    got_cot.wait()
    swaps[7].wait_recv()
    d_att = dot_t(cot_v[...], outw_v[...].reshape(HV, D)).astype(BF16)
    datt_v[y, x] = d_att
    dext_l = edge_copy(datt_v.at[y, x], datt_v.at[4, 1], left, edge_left)
    dext_r = edge_copy(datt_v.at[y, x], datt_v.at[4, 0], right, edge_right)

    for g in kv_g:
        g()
    kv_f = [kv_second(0), kv_second(1)]
    q_f = [q_first(0), q_first(1)]
    d_f = [d_first(0), d_first(1)]
    d_stack = stack_heads(d_att, VAL)
    kv_g = [f() for f in kv_f]
    q_g = [f() for f in q_f]
    d_g = [f() for f in d_f]
    edge_wait(ext_r, edge_right, edge_left)
    edge_wait(ext_l, edge_left, edge_right)
    for g in kv_g:
        g()
    for g in q_g + d_g:
        g()
    q_f = [q_second(0), q_second(1)]
    d_f = [d_second(0), d_second(1)]

    allowed = mask_q[...] > 0.5
    scale = KEY ** (-0.5)
    d_query = []
    stats = []
    for n in range(NS):
        k_all = proj_v[n, :, :, :, pl.ds(HK, HK)].reshape(CELLS, HK)
        v_all = proj_v[n, :, :, :, pl.ds(2 * HK, HV)].reshape(CELLS, HV)
        q_stack = stack_heads(proj[n * BINS : (n + 1) * BINS, :HK], KEY)
        score = jnp.where(allowed, dot_t(k_all, q_stack) * scale, -1e30)
        top = jnp.max(score, axis=0, keepdims=True)
        e = jnp.where(allowed, jnp.exp(score - top), 0.0)
        total = jnp.sum(e, axis=0, keepdims=True)
        prob = e / total
        d_prob = dot_t(v_all, d_stack)
        delta = jnp.sum(prob.astype(BF16).astype(F32) * d_prob, axis=0, keepdims=True)
        d_score = (prob * (d_prob - delta) * scale).astype(BF16)
        d_query.append(unstack_heads(dot_l(d_score, k_all), KEY))
        stats.append((top + jnp.log(total), delta))
    line = lax.broadcasted_iota(jnp.int32, (8, 128), 0)
    table = jnp.zeros((8, 128), F32)
    for n in range(NS):
        table = jnp.where(line == n, jnp.broadcast_to(stats[n][0], (8, 128)), table)
        table = jnp.where(line == 2 + n, jnp.broadcast_to(stats[n][1], (8, 128)), table)
    stat_v[y, x] = table
    stat_copies = []
    for dy in range(4):
        for dx in range(4):
            if dy or dx:
                stat_copies.append(
                    send(stat_v.at[y, x], stat_v.at[y, x], (sa, ((y + dy) % 4) * 4 + (x + dx) % 4, hi))
                )
    sext_l = edge_copy(stat_v.at[y, x], stat_v.at[4, 1], left, edge_left)
    sext_r = edge_copy(stat_v.at[y, x], stat_v.at[4, 0], right, edge_right)

    q_g = [f() for f in q_f]
    d_g = [f() for f in d_f]
    edge_wait(dext_r, edge_right, edge_left)
    edge_wait(dext_l, edge_left, edge_right)
    for g in q_g + d_g:
        g()

    allowed_k = mask_k[...] > 0.5
    d_all = datt_v[...].reshape(CELLS, HV)
    score_k, d_prob_k, q_alls = [], [], []
    for n in range(NS):
        q_all = proj_v[n, :, :, :, pl.ds(0, HK)].reshape(CELLS, HK)
        own = proj[n * BINS : (n + 1) * BINS]
        score_k.append(dot_t(stack_heads(own[:, HK : 2 * HK], KEY), q_all) * scale)
        d_prob_k.append(dot_t(stack_heads(own[:, 2 * HK :], VAL), d_all))
        q_alls.append(q_all)
    for copy in stat_copies:
        copy.wait_recv()
    edge_wait(sext_r, edge_right, edge_left)
    edge_wait(sext_l, edge_left, edge_right)
    cells = stat_v[...]
    lanes = lax.broadcasted_iota(jnp.int32, (8, 128), 1)
    by_head = []
    for h in range(HEADS):
        groups = []
        for g in range(5):
            part = jnp.zeros((8, 128), F32)
            for k in range(4):
                only = jnp.where(lanes // BINS == h, cells[g, k], 0.0)
                shift = (BINS * (k - h)) % 128
                part = part + (pltpu.roll(only, shift, 1) if shift else only)
            groups.append(part)
        by_head.append(jnp.concatenate(groups, axis=1))

    def spread(r):
        return jnp.concatenate([jnp.broadcast_to(by_head[h][r : r + 1], (BINS, CELLS)) for h in range(HEADS)], axis=0)

    pieces = []
    for n in range(NS):
        prob_k = jnp.where(allowed_k, jnp.exp(score_k[n] - spread(n)), 0.0)
        d_val = unstack_heads(dot(prob_k.astype(BF16), d_all), VAL)
        d_sk = (prob_k * (d_prob_k[n] - spread(2 + n)) * scale).astype(BF16)
        d_key = unstack_heads(dot(d_sk, q_alls[n]), KEY)
        pieces.append(jnp.concatenate([d_query[n], d_key, d_val], axis=1).astype(BF16))
    d_proj = jnp.concatenate(pieces, axis=0)

    gained = gain * dot_t(d_proj, qkv_v[...].reshape(D, QKV))
    resid = resid_v[...]
    cot = cot_v[...].astype(F32)
    mean = jnp.mean(resid * gained, axis=1, keepdims=True)
    d_resid = (
        jnp.concatenate([cot, cot], axis=0)
        + inv_rms * gained
        - resid * (inv_rms * inv_rms * inv_rms * mean)
    )
    d_act = dot_t(d_resid.astype(BF16), mix_v[...].reshape(HID, D))
    hg = (d_act * hidden_slope).astype(BF16)
    for n in range(NS):
        hgext[n, pl.ds(DIL, BINS), :] = hg[n * BINS : (n + 1) * BINS]
    back_l = edge_copy(hgext.at[:, pl.ds(DIL, DIL), :], hgext.at[:, pl.ds(DIL + BINS, DIL), :], left, has_left)
    back_r = edge_copy(hgext.at[:, pl.ds(BINS, DIL), :], hgext.at[:, pl.ds(0, DIL), :], right, has_right)
    resid_v[...] = d_resid
    edge_wait(back_r, has_right, has_left)
    edge_wait(back_l, has_left, has_right)

    finals = []
    for chunk in range(2):
        c = pl.ds(chunk * 768, 768)
        grad_in = jnp.zeros((ROWS, 768), F32)
        for t in range(3):
            grad_in = grad_in + dot_t(tap_of(hgext, 2 - t), conv_v[t, pl.ds(chunk * 4, 4)].reshape(768, HID))
        grad = resid_v[:, c] + grad_in * slope_v[:, c]
        sum_v[:, c] = (grad[:BINS] + grad[BINS:]).astype(BF16)
        finals.append((c, send(sum_v.at[:, c], far_v.at[:, c], partner)))
    for c, copy in finals:
        copy.wait_recv()
        out_ref[:, c] = (sum_v[:, c].astype(F32) + far_v[:, c].astype(F32)) * 0.25
    for copy in pending:
        copy.wait_send()


def shards(base, noise, cot, convolution_weight, mix_w, norm_gain, qkv_w, out_w, band_width, pairs):
    anywhere = pl.BlockSpec(memory_space=pl.ANY)
    vmem = pl.BlockSpec(memory_space=pltpu.VMEM)
    smem = pl.BlockSpec(memory_space=pltpu.SMEM)
    return pl.pallas_call(
        kernel,
        out_shape=jax.ShapeDtypeStruct((BINS, D), F32),
        in_specs=[anywhere, anywhere, anywhere, anywhere, anywhere, vmem, anywhere, anywhere, smem, vmem],
        out_specs=vmem,
        scratch_shapes=[
            pltpu.VMEM((BINS, D), BF16),
            pltpu.VMEM((NS, BINS, D), BF16),
            pltpu.VMEM((BINS, D), BF16),
            pltpu.VMEM((ROWS, D), F32),
            pltpu.VMEM((ROWS, D), F32),
            pltpu.VMEM((NS, BINS + 2 * DIL, D), BF16),
            pltpu.VMEM((3, 8, 2, 4, 24, HID), BF16),
            pltpu.VMEM((8, 2, 24, D), BF16),
            pltpu.VMEM((8, 2, 4, 24, QKV), BF16),
            pltpu.VMEM((8, 2, 24, D), BF16),
            pltpu.VMEM((ROWS, D), F32),
            pltpu.VMEM((NS, 5, 4, BINS, QKV), BF16),
            pltpu.VMEM((5, 4, BINS, HV), BF16),
            pltpu.VMEM((5, 4, 8, 128), F32),
            pltpu.VMEM((CELLS, 128), F32),
            pltpu.VMEM((128, CELLS), F32),
            pltpu.VMEM((NS, BINS + 2 * DIL, HID), BF16),
            pltpu.VMEM((BINS, D), BF16),
            pltpu.VMEM((BINS, D), BF16),
            pltpu.SemaphoreType.DMA((NSEM,)),
            pltpu.SemaphoreType.DMA((NSEM,)),
            pltpu.SemaphoreType.DMA((16,)),
        ],
        compiler_params=pltpu.CompilerParams(
            collective_id=0, has_side_effects=True, vmem_limit_bytes=50 * 1024 * 1024
        ),
    )(
        base, noise, cot, convolution_weight, mix_w, norm_gain.reshape(1, D), qkv_w, out_w, band_width, pairs
    )


def solution(mesh):
    return jax.shard_map(
        shards,
        mesh=mesh,
        in_specs=(
            P(("sa", "sb"), None),
            P("noise", ("sa", "sb"), None),
            P(("sa", "sb"), None),
            P(None, "sa", None),
            P("sa", None),
            P(),
            P("sa", None),
            P("sa", None),
            P(),
            P(),
        ),
        out_specs=P(("sa", "sb"), None),
        check_vma=False,
    )
```

time: 634 us -> 117 us (0.18)
  the two profiles are of different devices: /device:TPU:1 before, /device:TPU:97 now
where the time goes in v1:
time: 117 us
  Pallas kernels  108 us (92%)
  local copies, waits for them, and re-layouts  8.38 us (7%)
    pallas_call x1, Pallas kernels, shards(): pl.pallas_call(kernel, out_shape=jax.ShapeDtypeStruct((BINS, D), F32), in...  108 us
    unnamed x20, local copies, waits for them, and re-layouts  7.67 us

profile of v1, /device:TPU:97, one launch (start us, length us, event | category | flops | bytes accessed | tf_op | source)
XLA Modules:
  0.0 116.6 jit_solution(1721363919470307813)
XLA Ops:
  0.0 0.0 copy-start.8
  0.0 0.7 reshape.3.gain_ref
  0.7 0.0 copy-done.8
  0.7 0.0 copy-start.7
  0.7 0.1 copy.11.pairs_ref
  0.8 0.6 copy-done.7
  1.4 0.0 copy-start
  1.4 0.9 copy-done
  2.3 0.0 copy-start.1
  2.3 0.9 copy-done.1
  3.2 0.0 copy-start.2
  3.2 0.9 copy-done.2
  4.2 0.0 copy-start.3
  4.2 0.9 copy-done.3
  5.1 0.0 copy-start.4
  5.1 0.9 copy-done.4
  5.9 0.0 copy-start.5
  5.9 0.9 copy-done.5
  6.8 0.0 copy-start.6
  6.8 0.9 copy-done.6
  7.7 108.2 %shard_map.100 = f32[32,1536]{1,0:T(8,128)S(1)} custom-call(bf16[32,1536]{1,0:T(8,128)(2,1)S(1)} %copy-done.3, bf16[2,32,1536]{2,1,0:T(8,128)(2,1)S(1)} %copy-done.1, bf16[32,1536]{1,0:T(8,128)(2,1)S(1)} %copy-done.4, bf16[3,96,384]{2,1,0:T(8,128)(2,1)S(1)} %copy-done, bf16[24,1536]{1,0:T(8,128)(2,1)S(1)} %copy-done.5, f32[1,1536]{1,0:T(1,128)S(1)} %reshape.3.gain_ref, ...), custom_call_target="tpu_custom_call" | custom-call | tf_op jit(solution)/shard_map/pallas_call | solution.py:569
  115.9 0.7 copy.13
Async XLA Ops:
  0.0 0.7 copy-start.8
  0.7 0.7 copy-start.7
  1.4 0.9 copy-start
  2.3 0.9 copy-start.1
  3.2 0.9 copy-start.2
  4.2 0.9 copy-start.3
  5.1 0.9 copy-start.4
  5.9 0.9 copy-start.5
  6.8 0.9 copy-start.6
